TPU v7x, 32 devices: a whole 2x2x4 slice. The times are simulated.
32 devices in a mesh: ens: 4 (over x, core), space: 8 (over z, y).
Axes of the slice: x: 2, y: 2, z: 4, core: 2. Of those that a mesh axis runs over, the one named last changes fastest.
Arguments:
- latents: bfloat16 [8, 32, 256, 256], P('ens', None, 'space'), may hold values from -6 to 6
- targets: bfloat16 [32, 256, 256], P(None, 'space'), may hold values from -6 to 6
- kernel: bfloat16 [3, 3, 256, 256], replicated, may hold values from -0.125 to 0.125
Outputs:
- loss: float32 [], replicated
- grad_input: bfloat16 [8, 32, 256, 256], P('ens', None, 'space')
- grad_kernel: float32 [3, 3, 256, 256], replicated
All inputs are finite; a program needn't handle non-finite values.
Results may differ from a plain program's by a relative error of at most 0.0047.
Values may be sent and summed in bfloat16 or wider, within the bound.
A program may use at most 64 MiB of HBM per device.

v0:
```python
import jax
import jax.numpy as jnp
from jax import lax
from jax.sharding import PartitionSpec as P

smoothing = 0.1


def padded_2(block, sides, width):
    for axis, dim in sides:
        count = lax.axis_size(axis)
        forward = [(i, i + 1) for i in range(count - 1)]
        forward.append((count - 1, 0))
        backward = [(target, source) for source, target in forward]
        low = lax.ppermute(
            lax.slice_in_dim(block, block.shape[dim] - width, None, axis=dim), axis, forward
        )
        high = lax.ppermute(lax.slice_in_dim(block, 0, width, axis=dim), axis, backward)
        block = jnp.concatenate([low, block, high], axis=dim)
    return block


def lat_pad(field):
    return jnp.pad(field, ((0, 0), (1, 1), (0, 0), (0, 0)))


def conv_forward(padded, kernel, rows, cols):
    chans = padded.shape[3]
    total = None
    for row_off in range(3):
        for col_off in range(3):
            window = padded[:, row_off : row_off + rows, col_off : col_off + cols, :].reshape(
                -1, chans
            )
            term = jnp.dot(window, kernel[row_off, col_off], preferred_element_type=jnp.float32)
            total = term if total is None else total + term
    return total.reshape(padded.shape[0], rows, cols, -1)


def conv_adjoint(padded, kernel, rows, cols):
    chans = padded.shape[3]
    total = None
    for row_off in range(3):
        for col_off in range(3):
            window = padded[
                :, 2 - row_off : 2 - row_off + rows, 2 - col_off : 2 - col_off + cols, :
            ].reshape(-1, chans)
            term = lax.dot_general(
                window,
                kernel[row_off, col_off],
                (((1,), (1,)), ((), ())),
                preferred_element_type=jnp.float32,
            )
            total = term if total is None else total + term
    return total.reshape(padded.shape[0], rows, cols, -1)


def kernel_terms(padded, slopes, rows, cols):
    chans = padded.shape[3]
    flat_slopes = slopes.reshape(-1, slopes.shape[3])
    blocks = []
    for row_off in range(3):
        for col_off in range(3):
            window = padded[:, row_off : row_off + rows, col_off : col_off + cols, :].reshape(
                -1, chans
            )
            blocks.append(
                lax.dot_general(
                    window,
                    flat_slopes,
                    (((0,), (0,)), ((), ())),
                    preferred_element_type=jnp.float32,
                )
            )
    return jnp.stack(blocks).reshape(3, 3, chans, -1)


def local(latents, targets, kernel):
    members_dev, rows, cols, chans = latents.shape
    members = members_dev * lax.axis_size("ens")
    longitude = cols * lax.axis_size("space")
    rimmed = padded_2(latents, (("space", 2),), 1)
    padded = lat_pad(rimmed)
    fields = conv_forward(padded, kernel, rows, cols)
    offset = fields - targets.astype(jnp.float32)[None]
    spread = jnp.sqrt(offset * offset + smoothing * smoothing)
    own_total = jnp.sum(spread)
    own_slope = offset / spread
    block = lax.all_to_all(fields, "ens", split_axis=1, concat_axis=0, tiled=True)
    gap = block[:, None] - block[None]
    width = jnp.sqrt(gap * gap + smoothing * smoothing)
    slope = jnp.sum(gap / width, axis=1)
    returned = lax.all_to_all(slope, "ens", split_axis=0, concat_axis=1, tiled=True)
    part_total = jnp.sum(width, axis=(0, 1))[None] - block.shape[0] * smoothing
    pair_total = jnp.sum(part_total)
    slopes = (own_slope / members - returned / (members * (members - 1))).astype(jnp.bfloat16)
    cell_sum = own_total / members - pair_total / (2 * members * (members - 1))
    slope_rimmed = padded_2(slopes, (("space", 2),), 1)
    grad_input = conv_adjoint(lat_pad(slope_rimmed), kernel, rows, cols).astype(jnp.bfloat16)
    partial_kernel = kernel_terms(padded, slopes, rows, cols) / (members * rows * longitude)
    grad_kernel, loss_total = lax.psum((partial_kernel, cell_sum), ("ens", "space"))
    loss = loss_total / (rows * longitude * chans)
    return (loss, grad_input, grad_kernel)


def solution(mesh):
    in_specs = (P("ens", None, "space", None), P(None, "space", None), P())
    out_specs = (P(), P("ens", None, "space", None), P())
    return jax.shard_map(local, mesh=mesh, in_specs=in_specs, out_specs=out_specs, check_vma=False)
```

profile of v0, /device:TPU:0, one launch (start us, length us, event | category | flops | bytes accessed | tf_op | source)
XLA Modules:
  0.0 301.2 jit_solution(1788002785526001829)
XLA Ops:
  7.2 1.2 fusion.72
  8.4 3.0 %collective-permute-start = (bf16[2,32,1,256]{3,2,1,0:T(2,128)(2,1)S(1)}, bf16[2,32,1,256]{3,2,1,0:T(2,128)(2,1)S(1)}, u32[]{:S(2)}, u32[]{:S(2)}) collective-permute-start(bf16[2,32,1,256]{3,2,1,0:T(2,128)(2,1)S(1)} %get-tuple-element.25), channel_id=1, source_target_pairs={{0,1},{1,2},{2,3},{3,4},{4,5},{5,6},{6,7},{7,0},{8,9},{9,10},{10,1... | collective-permute-start | bytes 98312 | tf_op jit(solution)/shard_map/ppermute | solution.py:15
  11.4 3.1 %collective-permute-start.1 = (bf16[2,32,1,256]{3,2,1,0:T(2,128)(2,1)S(1)}, bf16[2,32,1,256]{3,2,1,0:T(2,128)(2,1)S(1)}, u32[]{:S(2)}, u32[]{:S(2)}) collective-permute-start(bf16[2,32,1,256]{3,2,1,0:T(2,128)(2,1)S(1)} %get-tuple-element.26), channel_id=1, source_target_pairs={{1,0},{2,1},{3,2},{4,3},{5,4},{6,5},{7,6},{0,7},{9,8},{10,9},{11,1... | collective-permute-start | bytes 98312 | tf_op jit(solution)/shard_map/ppermute | solution.py:18
  14.5 1.7 fusion.33
  16.2 0.6 collective-permute-done
  16.8 0.3 collective-permute-done.1
  17.1 0.8 select_maximum_fusion.2
  17.9 1.0 fusion.70
  18.9 0.3 copy-done.9
  19.2 0.4 fusion.27
  19.6 0.4 fusion.43
  20.1 0.4 convolution_add_fusion.11
  20.5 0.4 convolution_add_fusion.10
  20.9 1.2 pad_maximum_fusion.2
  22.2 0.4 fusion.8
  22.6 0.5 copy-done.5
  23.1 0.4 copy-done.3
  23.5 0.4 fusion.7
  23.9 0.4 convolution_add_fusion.7
  24.3 0.4 convolution_add_fusion.6
  24.9 28.3 %all_to_all.24 = f32[2,32,32,256]{3,2,0,1:T(8,128)S(1)} all-to-all(f32[2,32,32,256]{3,2,0,1:T(8,128)S(1)} %copy.19), channel_id=1, replica_groups=mesh['ens'=4,'space'=8] {'ens'}, dimensions={1} | all-to-all | bytes 4194304 | tf_op jit(solution)/shard_map/all_to_all | solution.py:89
  53.2 0.2 copy.21
  53.4 9.9 %fusion.3 = (f32[8,8,32,256]{3,2,1,0:T(8,128)}, f32[8,32,256]{2,1,0:T(8,128)}) fusion(f32[8,8,32,256]{3,2,1,0:T(8,128)S(1)} %bitcast.208), kind=kLoop, calls=%fused_computation.5 | loop fusion | flops 24576000 | bytes 4456448 | tf_op jit(solution)/shard_map/reduce_sum | solution.py:92
  63.4 4.4 %all-to-all-start.1 = ((f32[8,8,32,256]{3,2,1,0:T(8,128)}), f32[8,8,32,256]{3,2,1,0:T(8,128)}, u32[]{:S(2)}, u32[]{:S(2)}) async-start(f32[8,8,32,256]{3,2,1,0:T(8,128)} %get-tuple-element.3), calls=%async_computation.1 | async-start | bytes 4194304 | tf_op jit(solution)/shard_map/all_to_all | solution.py:93
  67.8 0.2 all-reduce.4.cloned.1.call-start
  68.1 2.1 convert_element_type.18
  70.2 1.6 add_reduce_fusion
  72.5 21.1 %all-to-all-done.1 = f32[8,8,32,256]{3,2,1,0:T(8,128)} async-done(((f32[8,8,32,256]{3,2,1,0:T(8,128)}), f32[8,8,32,256]{3,2,1,0:T(8,128)}, u32[]{:S(2)}, u32[]{:S(2)}) %all-to-all-start.1) | async-done | bytes 2097184 | tf_op jit(solution)/shard_map/all_to_all | solution.py:93
  93.6 1.8 broadcast_multiply_fusion.1
  95.4 0.2 copy.22
  95.7 1.0 copy-done.7
  96.6 2.8 fusion.10
  99.4 2.3 subtract_convert_fusion
  101.6 0.8 fusion.71
  102.4 0.5 fusion.20
  102.9 1.1 collective-permute-start.2
  103.9 3.7 %collective-permute-start.3 = (bf16[2,32,1,256]{3,2,1,0:T(2,128)(2,1)}, bf16[2,32,1,256]{3,2,1,0:T(2,128)(2,1)}, u32[]{:S(2)}, u32[]{:S(2)}) collective-permute-start(bf16[2,32,1,256]{3,2,1,0:T(2,128)(2,1)} %get-tuple-element.22), channel_id=1, source_target_pairs={{1,0},{2,1},{3,2},{4,3},{5,4},{6,5},{7,6},{0,7},{9,8},{10,9},{11,1... | collective-permute-start | bytes 98312 | tf_op jit(solution)/shard_map/ppermute | solution.py:18
  107.6 0.5 fusion.19
  108.2 0.5 fusion.18
  108.6 0.7 copy-done.6
  109.4 0.5 fusion.17
  109.9 0.5 fusion.16
  110.4 0.3 copy-done.4
  110.7 0.5 fusion.15
  111.2 0.5 fusion.14
  111.7 0.5 fusion.13
  112.1 0.5 fusion.12
  112.7 1.6 broadcast_multiply_fusion
  114.9 0.2 copy-done.11
  115.1 1.8 fusion.31
  116.8 37.0 %psum.14 = f32[]{:T(128)} all-reduce(f32[]{:T(128)S(6)} %sub.50), channel_id=1, replica_groups=mesh['ens'=4,'space'=8] {'ens','space'}, use_global_device_ids=true, to_apply=%region_3.4 | all-reduce | flops 1 | bytes 8 | tf_op jit(solution)/shard_map/psum | solution.py:101
  154.6 1.7 select_maximum_fusion
  156.3 1.0 fusion.69
  157.2 0.5 fusion.41
  157.7 0.5 convolution_add_fusion.5
  158.2 0.5 convolution_add_fusion.4
  158.7 2.1 pad_maximum_fusion
  160.8 0.5 fusion.6
  161.2 0.5 fusion.25
  161.7 0.5 fusion.5
  162.2 0.5 convolution_add_fusion.1
  162.7 1.4 fusion.9
  164.1 125.8 %all-reduce.4.cloned.1.call-done = f32[3,3,256,256]{3,2,1,0:T(8,128)} async-done(((f32[3,3,256,256]{3,2,1,0:T(8,128)}), f32[3,3,256,256]{3,2,1,0:T(8,128)}) %all-reduce.4.cloned.1.call-update) | async-done | bytes 2359312 | tf_op jit(solution)/shard_map/psum | solution.py:101
  290.0 3.2 %copy.45 = f32[3,3,256,256]{3,2,1,0:T(8,128)} copy(f32[3,3,256,256]{3,2,1,0:T(8,128)} %all-reduce.4.cloned.1.call-done) | data formatting | bytes 4718592
  (21 shorter events, 0.2 us)
Async XLA Ops:
  7.2 9.9 %copy-start.1 = (bf16[2,32,32,256]{3,2,1,0:T(8,128)(2,1)S(1)}, bf16[2,32,32,256]{3,2,1,0:T(8,128)(2,1)}, u32[]{:S(2)}) copy-start(bf16[2,32,32,256]{3,2,1,0:T(8,128)(2,1)} %param.3) | copy-start | bytes 3145732
  8.4 8.4 %collective-permute-start = (bf16[2,32,1,256]{3,2,1,0:T(2,128)(2,1)S(1)}, bf16[2,32,1,256]{3,2,1,0:T(2,128)(2,1)S(1)}, u32[]{:S(2)}, u32[]{:S(2)}) collective-permute-start(bf16[2,32,1,256]{3,2,1,0:T(2,128)(2,1)S(1)} %get-tuple-element.25), channel_id=1, source_target_pairs={{0,1},{1,2},{2,3},{3,4},{4,5},{5,6},{6,7},{7,0},{8,9},{9,10},{10,1... | collective-permute-start | bytes 98312 | tf_op jit(solution)/shard_map/ppermute | solution.py:15
  11.4 5.7 %collective-permute-start.1 = (bf16[2,32,1,256]{3,2,1,0:T(2,128)(2,1)S(1)}, bf16[2,32,1,256]{3,2,1,0:T(2,128)(2,1)S(1)}, u32[]{:S(2)}, u32[]{:S(2)}) collective-permute-start(bf16[2,32,1,256]{3,2,1,0:T(2,128)(2,1)S(1)} %get-tuple-element.26), channel_id=1, source_target_pairs={{1,0},{2,1},{3,2},{4,3},{5,4},{6,5},{7,6},{0,7},{9,8},{10,9},{11,1... | collective-permute-start | bytes 98312 | tf_op jit(solution)/shard_map/ppermute | solution.py:18
  17.9 1.3 copy-start.9
  22.1 1.0 copy-start.5
  22.2 1.3 copy-start.3
  24.8 70.9 %copy-start = (f32[2048,256]{1,0:T(8,128)}, f32[2048,256]{1,0:T(8,128)S(1)}, u32[]{:S(2)}) copy-start(f32[2048,256]{1,0:T(8,128)S(1)} %convolution_add_fusion.6) | copy-start | bytes 6291460
  63.4 30.2 %all-to-all-start.1 = ((f32[8,8,32,256]{3,2,1,0:T(8,128)}), f32[8,8,32,256]{3,2,1,0:T(8,128)}, u32[]{:S(2)}, u32[]{:S(2)}) async-start(f32[8,8,32,256]{3,2,1,0:T(8,128)} %get-tuple-element.3), calls=%async_computation.1 | async-start | bytes 4194304 | tf_op jit(solution)/shard_map/all_to_all | solution.py:93
  67.8 222.1 %all-reduce.4.cloned.1.call-start = ((), (), s32[]{:S(2)}) async-start(), calls=%async_computation.2 | async-start | bytes 4718592 | tf_op jit(solution)/shard_map/psum | solution.py:101
  95.4 1.2 copy-start.7
  102.9 51.7 %collective-permute-start.2 = (bf16[2,32,1,256]{3,2,1,0:T(2,128)(2,1)}, bf16[2,32,1,256]{3,2,1,0:T(2,128)(2,1)S(1)}, u32[]{:S(2)}, u32[]{:S(2)}) collective-permute-start(bf16[2,32,1,256]{3,2,1,0:T(2,128)(2,1)} %get-tuple-element.21), channel_id=1, source_target_pairs={{0,1},{1,2},{2,3},{3,4},{4,5},{5,6},{6,7},{7,0},{8,9},{9,10},{10,1... | collective-permute-start | bytes 98312 | tf_op jit(solution)/shard_map/ppermute | solution.py:15
  103.9 50.6 %collective-permute-start.3 = (bf16[2,32,1,256]{3,2,1,0:T(2,128)(2,1)}, bf16[2,32,1,256]{3,2,1,0:T(2,128)(2,1)}, u32[]{:S(2)}, u32[]{:S(2)}) collective-permute-start(bf16[2,32,1,256]{3,2,1,0:T(2,128)(2,1)} %get-tuple-element.22), channel_id=1, source_target_pairs={{1,0},{2,1},{3,2},{4,3},{5,4},{6,5},{7,6},{0,7},{9,8},{10,9},{11,1... | collective-permute-start | bytes 98312 | tf_op jit(solution)/shard_map/ppermute | solution.py:18
  108.1 1.2 copy-start.6
  108.2 1.7 copy-start.2
  109.4 1.3 copy-start.4
  112.6 2.3 copy-start.10
  112.6 2.4 copy-start.11
  158.7 2.1 copy-start.8
Sparse Core Ops, SparseCore 0:
  154.0 135.8 all-reduce.3
where the time goes:
time: 302 us; the launch traced here: 301 us
  waiting for transfers between devices  148 us (49%)
  blocking collectives  65.3 us (22%)
  other arithmetic  27.9 us (9%)
  between operations  17.5 us (6%)
  matrix products  16 us (5%)
  starting transfers between devices  15.6 us (5%)
  local copies, waits for them, and re-layouts  11.1 us (4%)
    psum x1, waiting for transfers between devices, local(): lax.psum((partial_kernel, cell_sum), ('ens', 'space'))  126 us
    psum x1, blocking collectives, local(): lax.psum((partial_kernel, cell_sum), ('ens', 'space'))  37 us
    all_to_all x1, blocking collectives, local(): lax.all_to_all(fields, 'ens', split_axis=1, concat_axis=0, tiled=True)  28.3 us
    all_to_all x1, waiting for transfers between devices, local(): lax.all_to_all(slope, 'ens', split_axis=0, concat_axis=1, tiled=True)  21.1 us
    reduce_sum x1, other arithmetic, local(): slope = jnp.sum(gap / width, axis=1)  9.94 us
    ppermute x2, starting transfers between devices, padded_2(): lax.ppermute(lax.slice_in_dim(block, 0, width, axis=dim), axis, backward)  6.82 us
    unnamed x25, local copies, waits for them, and re-layouts  6.52 us
    dot_general x9, matrix products, conv_adjoint(): lax.dot_general(window, kernel[row_off, col_off], (((1,), (1,)), ((), ())...  6.51 us
  transfers between devices with their start and end apart: 6, of which 4 were waited for; matrix products, arithmetic and copies ran while one was open for 7% of the time, Pallas kernels for 0%

commit v1 on v0

--- a/solution.py
+++ b/solution.py
@@ -98,7 +98,7 @@
     slope_rimmed = padded_2(slopes, (("space", 2),), 1)
     grad_input = conv_adjoint(lat_pad(slope_rimmed), kernel, rows, cols).astype(jnp.bfloat16)
     partial_kernel = kernel_terms(padded, slopes, rows, cols) / (members * rows * longitude)
-    grad_kernel, loss_total = lax.psum((partial_kernel, cell_sum), ("ens", "space"))
+    grad_kernel, loss_total = lax.psum(lax.psum((partial_kernel, cell_sum), "space"), "ens")
     loss = loss_total / (rows * longitude * chans)
     return (loss, grad_input, grad_kernel)
 

time: 302 us -> 318 us (1.053)
  matrix products: 16 us -> 27.5 us
  blocking collectives: 65.3 us -> 57.3 us
  waiting for transfers between devices: 148 us -> 156 us
    psum x1 -> x2, waiting for transfers between devices: 126 us -> 134 us  [the longest x1 82.6 us: local(): lax.psum((partial_kernel, cell_sum), 'space')]
    psum x1 -> x2, blocking collectives: 37 us -> 29 us  [the longest x1 22.1 us: local(): lax.psum((partial_kernel, cell_sum), 'space')]
    dot_general x9, matrix products: 4.37 us -> 10.7 us  [kernel_terms(): lax.dot_general(window, flat_slopes, (((0,), (0,)), ((), ())), preferred_...]
    dot_general x9, matrix products: 6.51 us -> 11.7 us  [conv_adjoint(): lax.dot_general(window, kernel[row_off, col_off], (((1,), (1,)), ((), ())...]
    unnamed x25 -> x31, local copies, waits for them, and re-layouts: 6.52 us -> 8.51 us
  transfers between devices with their start and end apart: 6 -> 7, of which waited for: 4 -> 5; matrix products, arithmetic and copies ran while one was open for 7% -> 11% of each run, Pallas kernels for 0% -> 0%
where the time goes in v1:
time: 318 us; the launch traced here: 317 us
  waiting for transfers between devices  156 us (49%)
  blocking collectives  57.3 us (18%)
  other arithmetic  28.7 us (9%)
  matrix products  27.5 us (9%)
  between operations  17.4 us (5%)
  starting transfers between devices  15.6 us (5%)
  local copies, waits for them, and re-layouts  14.1 us (4%)
    psum x1, waiting for transfers between devices, local(): lax.psum((partial_kernel, cell_sum), 'space')  82.6 us
    psum x1, waiting for transfers between devices, local(): lax.psum(lax.psum((partial_kernel, cell_sum), 'space'), 'ens')  51.5 us
    all_to_all x1, blocking collectives, local(): lax.all_to_all(fields, 'ens', split_axis=1, concat_axis=0, tiled=True)  28.3 us
    psum x1, blocking collectives, local(): lax.psum((partial_kernel, cell_sum), 'space')  22.1 us
    all_to_all x1, waiting for transfers between devices, local(): lax.all_to_all(slope, 'ens', split_axis=0, concat_axis=1, tiled=True)  21.1 us
    dot_general x9, matrix products, conv_adjoint(): lax.dot_general(window, kernel[row_off, col_off], (((1,), (1,)), ((), ())...  11.7 us
    dot_general x9, matrix products, kernel_terms(): lax.dot_general(window, flat_slopes, (((0,), (0,)), ((), ())), preferred_...  10.7 us
    reduce_sum x1, other arithmetic, local(): slope = jnp.sum(gap / width, axis=1)  9.94 us
  transfers between devices with their start and end apart: 7, of which 5 were waited for; matrix products, arithmetic and copies ran while one was open for 11% of the time, Pallas kernels for 0%

profile of v1, /device:TPU:0, one launch (start us, length us, event | category | flops | bytes accessed | tf_op | source)
XLA Modules:
  0.0 316.7 jit_solution(5856451937051660011)
XLA Ops:
  7.2 1.2 fusion.72
  8.4 3.0 collective-permute-start
  11.4 3.1 collective-permute-start.1
  14.5 1.7 fusion.33
  16.2 0.6 collective-permute-done
  16.8 0.3 collective-permute-done.1
  17.1 0.8 select_maximum_fusion.2
  17.9 1.0 fusion.70
  18.9 0.3 copy-done.9
  19.2 0.4 fusion.27
  19.6 0.4 fusion.43
  20.1 0.4 convolution_add_fusion.11
  20.5 0.4 convolution_add_fusion.10
  20.9 1.2 pad_maximum_fusion.2
  22.2 0.4 fusion.8
  22.6 0.5 copy-done.5
  23.1 0.4 copy-done.3
  23.5 0.4 fusion.7
  23.9 0.4 convolution_add_fusion.7
  24.3 0.4 convolution_add_fusion.6
  24.9 28.3 %all_to_all.24 = f32[2,32,32,256]{3,2,0,1:T(8,128)S(1)} all-to-all(f32[2,32,32,256]{3,2,0,1:T(8,128)S(1)} %copy.19), channel_id=1, replica_groups=mesh['ens'=4,'space'=8] {'ens'}, dimensions={1} | all-to-all | bytes 4194304 | tf_op jit(solution)/shard_map/all_to_all | solution.py:89
  53.2 0.2 copy.21
  53.4 9.9 %fusion.3 = (f32[8,8,32,256]{3,2,1,0:T(8,128)}, f32[8,32,256]{2,1,0:T(8,128)}) fusion(f32[8,8,32,256]{3,2,1,0:T(8,128)S(1)} %bitcast.208), kind=kLoop, calls=%fused_computation.5 | loop fusion | flops 24576000 | bytes 4456448 | tf_op jit(solution)/shard_map/reduce_sum | solution.py:92
  63.4 4.4 %all-to-all-start.1 = ((f32[8,8,32,256]{3,2,1,0:T(8,128)}), f32[8,8,32,256]{3,2,1,0:T(8,128)}, u32[]{:S(2)}, u32[]{:S(2)}) async-start(f32[8,8,32,256]{3,2,1,0:T(8,128)} %get-tuple-element.3), calls=%async_computation.1 | async-start | bytes 4194304 | tf_op jit(solution)/shard_map/all_to_all | solution.py:93
  68.1 2.1 convert_element_type.18
  70.2 1.6 add_reduce_fusion
  72.5 21.1 %all-to-all-done.1 = f32[8,8,32,256]{3,2,1,0:T(8,128)} async-done(((f32[8,8,32,256]{3,2,1,0:T(8,128)}), f32[8,8,32,256]{3,2,1,0:T(8,128)}, u32[]{:S(2)}, u32[]{:S(2)}) %all-to-all-start.1) | async-done | bytes 2097184 | tf_op jit(solution)/shard_map/all_to_all | solution.py:93
  93.6 1.8 broadcast_multiply_fusion.1
  95.4 0.2 copy.22
  95.7 1.0 copy-done.7
  96.6 2.8 fusion.10
  99.4 2.3 subtract_convert_fusion
  101.6 1.2 fusion.20
  103.6 22.1 %psum.28 = f32[]{:T(128)} all-reduce(f32[]{:T(128)S(6)} %sub.50), channel_id=1, replica_groups=mesh['ens'=4,'space'=8] {'space'}, use_global_device_ids=true, to_apply=%region_3.4 | all-reduce | flops 1 | bytes 8 | tf_op jit(solution)/shard_map/psum | solution.py:101
  125.7 4.7 %collective-permute-start.3 = (bf16[2,32,1,256]{3,2,1,0:T(2,128)(2,1)S(1)}, bf16[2,32,1,256]{3,2,1,0:T(2,128)(2,1)S(1)}, u32[]{:S(2)}, u32[]{:S(2)}) collective-permute-start(bf16[2,32,1,256]{3,2,1,0:T(2,128)(2,1)S(1)} %get-tuple-element.22), channel_id=1, source_target_pairs={{1,0},{2,1},{3,2},{4,3},{5,4},{6,5},{7,6},{0,7},{9,8},{10,9},{11,1... | collective-permute-start | bytes 98312 | tf_op jit(solution)/shard_map/ppermute | solution.py:18
  130.4 1.2 fusion.19
  131.6 1.2 fusion.18
  132.9 1.2 fusion.17
  134.0 1.2 fusion.16
  135.3 1.2 fusion.15
  136.4 1.2 fusion.14
  137.6 1.2 fusion.13
  138.8 1.2 fusion.12
  140.0 3.3 %broadcast_multiply_fusion = f32[9,256,256]{2,1,0:T(8,128)} fusion(f32[9,256,256]{2,1,0:T(8,128)} %fusion.12), kind=kLoop, calls=%fused_computation.37 | loop fusion | flops 589824 | bytes 4718592 | tf_op jit(solution)/shard_map/div | solution.py:100
  143.3 1.1 copy-done.11
  144.5 2.7 fusion.31
  147.2 6.9 %psum.29 = f32[]{:T(128)} all-reduce(f32[]{:T(128)} %psum.28), channel_id=1, replica_groups=mesh['ens'=4,'space'=8] {'ens'}, use_global_device_ids=true, to_apply=%region_4.5 | all-reduce | flops 1 | bytes 8 | tf_op jit(solution)/shard_map/psum | solution.py:101
  154.8 2.1 pad_maximum_fusion
  156.9 0.8 select_maximum_fusion
  157.7 2.7 fusion.69
  160.4 1.4 fusion.41
  161.7 1.4 convolution_add_fusion.5
  163.1 1.5 convolution_add_fusion.4
  164.8 0.3 copy-done.10
  165.1 0.5 fusion.6
  165.7 82.6 %all-reduce.5.cloned.1.call-done = f32[3,3,256,256]{3,2,1,0:T(8,128)} async-done(((f32[3,3,256,256]{3,2,1,0:T(8,128)}), f32[3,3,256,256]{3,2,1,0:T(8,128)}) %all-reduce.5.cloned.1.call-update) | async-done | bytes 2359312 | tf_op jit(solution)/shard_map/psum | solution.py:101
  248.4 1.8 fusion.25
  250.2 0.5 fusion.5
  250.6 0.7 copy-done.14
  251.4 0.5 convolution_add_fusion.1
  251.9 0.7 copy-done.13
  252.6 1.4 fusion.9
  254.0 51.5 %all-reduce.7.cloned.1.call-done = f32[3,3,256,256]{3,2,1,0:T(8,128)} async-done(((f32[3,3,256,256]{3,2,1,0:T(8,128)}), f32[3,3,256,256]{3,2,1,0:T(8,128)}) %all-reduce.7.cloned.1.call-update) | async-done | bytes 2359312 | tf_op jit(solution)/shard_map/psum | solution.py:101
  305.5 3.2 %copy.46 = f32[3,3,256,256]{3,2,1,0:T(8,128)} copy(f32[3,3,256,256]{3,2,1,0:T(8,128)} %all-reduce.7.cloned.1.call-done) | data formatting | bytes 4718592
  (31 shorter events, 0.8 us)
Async XLA Ops:
  7.2 9.9 %copy-start.1 = (bf16[2,32,32,256]{3,2,1,0:T(8,128)(2,1)S(1)}, bf16[2,32,32,256]{3,2,1,0:T(8,128)(2,1)}, u32[]{:S(2)}) copy-start(bf16[2,32,32,256]{3,2,1,0:T(8,128)(2,1)} %param.3) | copy-start | bytes 3145732
  8.4 8.4 %collective-permute-start = (bf16[2,32,1,256]{3,2,1,0:T(2,128)(2,1)S(1)}, bf16[2,32,1,256]{3,2,1,0:T(2,128)(2,1)S(1)}, u32[]{:S(2)}, u32[]{:S(2)}) collective-permute-start(bf16[2,32,1,256]{3,2,1,0:T(2,128)(2,1)S(1)} %get-tuple-element.25), channel_id=1, source_target_pairs={{0,1},{1,2},{2,3},{3,4},{4,5},{5,6},{6,7},{7,0},{8,9},{9,10},{10,1... | collective-permute-start | bytes 98312 | tf_op jit(solution)/shard_map/ppermute | solution.py:15
  11.4 5.7 %collective-permute-start.1 = (bf16[2,32,1,256]{3,2,1,0:T(2,128)(2,1)S(1)}, bf16[2,32,1,256]{3,2,1,0:T(2,128)(2,1)S(1)}, u32[]{:S(2)}, u32[]{:S(2)}) collective-permute-start(bf16[2,32,1,256]{3,2,1,0:T(2,128)(2,1)S(1)} %get-tuple-element.26), channel_id=1, source_target_pairs={{1,0},{2,1},{3,2},{4,3},{5,4},{6,5},{7,6},{0,7},{9,8},{10,9},{11,1... | collective-permute-start | bytes 98312 | tf_op jit(solution)/shard_map/ppermute | solution.py:18
  17.9 1.3 copy-start.9
  22.1 1.0 copy-start.5
  22.2 1.3 copy-start.3
  24.8 70.9 %copy-start = (f32[2048,256]{1,0:T(8,128)}, f32[2048,256]{1,0:T(8,128)S(1)}, u32[]{:S(2)}) copy-start(f32[2048,256]{1,0:T(8,128)S(1)} %convolution_add_fusion.6) | copy-start | bytes 6291460
  63.4 30.2 %all-to-all-start.1 = ((f32[8,8,32,256]{3,2,1,0:T(8,128)}), f32[8,8,32,256]{3,2,1,0:T(8,128)}, u32[]{:S(2)}, u32[]{:S(2)}) async-start(f32[8,8,32,256]{3,2,1,0:T(8,128)} %get-tuple-element.3), calls=%async_computation.1 | async-start | bytes 4194304 | tf_op jit(solution)/shard_map/all_to_all | solution.py:93
  67.8 180.5 %all-reduce.5.cloned.1.call-start = ((), (), s32[]{:S(2)}) async-start(), calls=%async_computation.2 | async-start | bytes 4718592 | tf_op jit(solution)/shard_map/psum | solution.py:101
  95.4 1.2 copy-start.7
  125.7 29.0 %collective-permute-start.2 = (bf16[2,32,1,256]{3,2,1,0:T(2,128)(2,1)S(1)}, bf16[2,32,1,256]{3,2,1,0:T(2,128)(2,1)S(1)}, u32[]{:S(2)}, u32[]{:S(2)}) collective-permute-start(bf16[2,32,1,256]{3,2,1,0:T(2,128)(2,1)S(1)} %get-tuple-element.21), channel_id=1, source_target_pairs={{0,1},{1,2},{2,3},{3,4},{4,5},{5,6},{6,7},{7,0},{8,9},{9,10},{10,1... | collective-permute-start | bytes 98312 | tf_op jit(solution)/shard_map/ppermute | solution.py:15
  125.7 29.0 %collective-permute-start.3 = (bf16[2,32,1,256]{3,2,1,0:T(2,128)(2,1)S(1)}, bf16[2,32,1,256]{3,2,1,0:T(2,128)(2,1)S(1)}, u32[]{:S(2)}, u32[]{:S(2)}) collective-permute-start(bf16[2,32,1,256]{3,2,1,0:T(2,128)(2,1)S(1)} %get-tuple-element.22), channel_id=1, source_target_pairs={{1,0},{2,1},{3,2},{4,3},{5,4},{6,5},{7,6},{0,7},{9,8},{10,9},{11,1... | collective-permute-start | bytes 98312 | tf_op jit(solution)/shard_map/ppermute | solution.py:18
  131.6 1.2 copy-start.6
  131.6 2.4 copy-start.2
  132.9 2.4 copy-start.4
  143.3 1.2 copy-start.11
  143.3 162.3 %all-reduce.7.cloned.1.call-start = ((), (), s32[]{:S(2)}) async-start(), calls=%async_computation.3 | async-start | bytes 4718592 | tf_op jit(solution)/shard_map/psum | solution.py:101
  163.1 1.7 copy-start.8
  163.1 2.0 copy-start.10
  248.3 1.8 copy-start.12
  250.1 1.2 copy-start.14
  251.4 1.2 copy-start.13
Sparse Core Ops, SparseCore 0:
  143.4 104.8 all-reduce.4
  250.8 54.6 all-reduce.6
